TPU v7x, 32 devices: a whole 2x2x4 slice. The times are simulated.
32 devices in a mesh: dp: 8 (over y, x, core), tensor: 4 (over z).
Axes of the slice: x: 2, y: 2, z: 4, core: 2. Of those that a mesh axis runs over, the one named last changes fastest.
Arguments:
- acts: bfloat16 [3072, 4096], P('dp', 'tensor'), may hold values from -6 to 6
- grad_out: bfloat16 [3072, 4096], P('dp', 'tensor'), may hold values from -60 to 60
- gate_pre: bfloat16 [3072, 14336], P('dp', 'tensor'), may hold values from -6 to 6
- up_pre: bfloat16 [3072, 14336], P('dp', 'tensor'), may hold values from -6 to 6
- down_weight: bfloat16 [14336, 4096], P('tensor', 'dp'), may hold values from -0.09375 to 0.09375
- proj_in: bfloat16 [4096, 64], P('tensor'), may hold values from -0.09375 to 0.09375
- proj_out: bfloat16 [14336, 64], P('tensor'), may hold values from -0.046875 to 0.046875
- lengths: int32 [24], P('dp'), may hold values from 64 to 128
- query_ids: int32 [16], replicated, may hold values from 0 to 23
Outputs:
- gram: float32 [4096, 4096], P('dp', 'tensor')
- scores: float32 [16, 24], P(None, 'dp')
Inputs may be any that keep to these rules, and one draw needn't show every extreme that they name: `query_ids`: queries may repeat.
All inputs are finite; a program needn't handle non-finite values.
Results may differ from a plain program's by a relative error of at most 0.004.
Values may be sent and summed in bfloat16 or wider, within the bound.
A program may use at most 128 MiB of HBM per device.

v0:
```python
import jax
import jax.numpy as jnp
from jax import lax
from jax.sharding import PartitionSpec as P


def silu_slope(value):
    sigma = jax.nn.sigmoid(value)
    return sigma + value * sigma * (1.0 - sigma)


def body(acts, grad_out, gate_pre, up_pre, down_weight, proj_in, proj_out, lengths, query_ids):
    highest = lax.Precision.HIGHEST
    tokens_here = acts.shape[0]
    examples_here = lengths.shape[0]
    seq_len = tokens_here // examples_here
    full_grad = lax.all_gather(grad_out, "tensor", axis=1, tiled=True)
    hidden_grad = lax.dot_general(
        full_grad,
        lax.all_gather(down_weight, "dp", axis=1, tiled=True),
        (((1,), (1,)), ((), ())),
        preferred_element_type=jnp.float32,
    )
    gate_value = gate_pre.astype(jnp.float32)
    gate_grad = (hidden_grad * up_pre.astype(jnp.float32) * silu_slope(gate_value)).astype(
        jnp.bfloat16
    )
    out_part = jnp.dot(gate_grad, proj_out, preferred_element_type=jnp.float32)
    in_part = jnp.dot(acts, proj_in, preferred_element_type=jnp.float32)
    out_factor, in_factor = lax.psum((out_part, in_part), "tensor")
    positions = lax.broadcasted_iota(jnp.int32, (examples_here, seq_len), 1)
    live = (positions < lengths[:, None]).astype(jnp.float32)
    out_factor = out_factor.reshape(examples_here, seq_len, -1) * live[:, :, None]
    in_factor = in_factor.reshape(examples_here, seq_len, -1)
    features = jnp.einsum("esa,esb->eab", out_factor, in_factor, precision=highest).reshape(
        examples_here, -1
    )
    width = features.shape[1]
    first_example = lax.axis_index("dp") * examples_here
    example_ids = first_example + lax.broadcasted_iota(jnp.int32, (1, examples_here), 1)
    selector = (query_ids[:, None] == example_ids).astype(jnp.float32)
    query_part = jnp.dot(selector, features, precision=highest)
    local_square = jnp.sum(features * features)
    query_feat, total_square = lax.psum((query_part, local_square), "dp")
    examples_all = examples_here * lax.axis_size("dp")
    norm_mean = total_square / examples_all + 1e-06
    col_width = width // lax.axis_size("tensor")
    own_cols = lax.dynamic_slice_in_dim(
        features, lax.axis_index("tensor") * col_width, col_width, 1
    )
    row_block = lax.all_to_all(features, "dp", split_axis=1, concat_axis=0, tiled=True)
    block = lax.dot_general(
        row_block,
        lax.all_gather(own_cols, "dp", axis=0, tiled=True),
        (((0,), (0,)), ((), ())),
        precision=highest,
        preferred_element_type=jnp.float32,
    )
    gram = block * (width / examples_all) / norm_mean
    scores = jnp.dot(query_feat, features.T, precision=highest) / norm_mean
    return (gram, scores)


def solution(mesh):
    in_specs = (
        P("dp", "tensor"),
        P("dp", "tensor"),
        P("dp", "tensor"),
        P("dp", "tensor"),
        P("tensor", "dp"),
        P("tensor", None),
        P("tensor", None),
        P("dp"),
        P(),
    )
    out_specs = (P("dp", "tensor"), P(None, "dp"))
    return jax.shard_map(body, mesh=mesh, in_specs=in_specs, out_specs=out_specs, check_vma=False)
```

profile of v0, /device:TPU:0, one launch (start us, length us, event | category | flops | bytes accessed | tf_op | source)
XLA Modules:
  0.0 374.6 jit_solution(14562197754892564738)
XLA Ops:
  7.2 0.0 copy-start
  7.2 0.0 all-gather.4.cloned.1.call-start
  7.2 0.7 all-gather.4.cloned.1.call-update
  7.9 0.0 all-gather.6.cloned.1.call-start
  8.0 0.7 all-gather.6.cloned.1.call-update
  8.7 0.0 all-reduce.6.cloned.1.call-start
  8.8 0.4 convolution_bitcast_fusion
  9.1 0.6 copy.25
  9.8 66.0 %all-gather.4.cloned.1.call-done = bf16[384,4096]{1,0:T(8,128)(2,1)} async-done(((bf16[384,1024]{1,0:T(8,128)(2,1)}), bf16[384,4096]{1,0:T(8,128)(2,1)}) %all-gather.4.cloned.1.call-update) | async-done | bytes 3145744 | tf_op jit(solution)/shard_map/all_gather | solution.py:17
  75.8 149.3 %all-gather.6.cloned.1.call-done = bf16[3584,4096]{1,0:T(8,128)(2,1)} async-done(((bf16[3584,512]{1,0:T(8,128)(2,1)}), bf16[3584,4096]{1,0:T(8,128)(2,1)}) %all-gather.6.cloned.1.call-update) | async-done | bytes 29360144 | tf_op jit(solution)/shard_map/all_gather | solution.py:20
  225.1 0.0 copy-done.4
  225.1 20.3 %fusion.9 = f32[384,64]{0,1:T(8,128)S(1)} fusion(bf16[3584,64]{0,1:T(8,128)(2,1)S(1)} %copy-done.4, bf16[384,4096]{1,0:T(8,128)(2,1)} %all-gather.4.cloned.1.call-done, bf16[3584,4096]{1,0:T(8,128)(2,1)} %all-gather.6.cloned.1.call-done, bf16[384,3584]{1,0:T(8,128)(2,1)} %param.11, bf16[384,3584]{1,0:T(8,128)(2,1)} %param.12), kind=kOutput, calls=%fused_computation.17 | convolution fusion | flops 11466964992 | bytes 38567936 | tf_op jit(solution)/shard_map/dot_general | solution.py:28
  245.4 0.7 reshape.43
  246.1 0.0 all-reduce.6.cloned.1.call-update
  246.2 0.1 fusion.14
  246.2 35.4 %all-reduce.6.cloned.1.call-done = (f32[3,128,64]{1,2,0:T(8,128)}, f32[3,128,64]{1,0,2:T(4,128)}) async-done(((f32[3,128,64]{1,2,0:T(8,128)}, f32[3,128,64]{1,0,2:T(4,128)}), (f32[3,128,64]{1,2,0:T(8,128)}, f32[3,128,64]{1,0,2:T(4,128)})) %all-reduce.6.cloned.1.call-update) | async-done | bytes 196624 | tf_op jit(solution)/shard_map/psum | solution.py:30
  281.6 0.9 broadcast_multiply_fusion
  282.5 1.8 multiply_reduce_fusion
  284.3 0.1 all_to_all.14
  284.4 0.1 reshape.45
  284.5 0.7 copy.18
  285.2 3.6 all-to-all-start
  288.8 0.0 all-reduce.4.cloned.1.call-start
  288.8 1.0 fusion.10
  289.9 15.0 %psum.30 = f32[]{:T(128)} all-reduce(f32[]{:T(128)} %get-tuple-element.4), channel_id=1, replica_groups=mesh['dp'=8,'tensor'=4] {'dp'}, use_global_device_ids=true, to_apply=%region_3.0 | all-reduce | flops 1 | bytes 8 | tf_op jit(solution)/shard_map/psum | solution.py:44
  304.9 8.2 %all-gather = f32[8,3,1024]{2,1,0:T(4,128)S(1)} all-gather(f32[1,3,1024]{2,1,0:T(4,128)S(1)} %dynamic-slice_bitcast_fusion), channel_id=1, replica_groups=mesh['dp'=8,'tensor'=4] {'dp'}, dimensions={0}, use_global_device_ids=true | all-gather | bytes 110592 | tf_op jit(solution)/shard_map/all_gather | solution.py:54
  313.1 0.1 reshape.47
  313.2 0.0 all-reduce.4.cloned.1.call-update
  313.8 0.0 all-to-all-done
  313.9 3.2 multiply_divide_fusion
  317.1 49.0 %all-reduce.4.cloned.1.call-done = f32[16,4096]{1,0:T(8,128)} async-done(((f32[16,4096]{1,0:T(8,128)}), f32[16,4096]{1,0:T(8,128)}) %all-reduce.4.cloned.1.call-update) | async-done | bytes 262160 | tf_op jit(solution)/shard_map/psum | solution.py:44
  366.1 2.0 convolution_divide_fusion
  (11 shorter events, 0.0 us)
Async XLA Ops:
  7.2 1.6 copy-start
  7.2 1.6 copy-start.1
  7.2 217.9 %copy-start.4 = (bf16[3584,64]{0,1:T(8,128)(2,1)S(1)}, bf16[3584,64]{0,1:T(8,128)(2,1)}, u32[]{:S(2)}) copy-start(bf16[3584,64]{0,1:T(8,128)(2,1)} %param.15) | copy-start | bytes 1376260
  7.2 68.6 %all-gather.4.cloned.1.call-start = ((), (), s32[]{:S(2)}) async-start(), calls=%async_computation.1 | async-start | bytes 3932160 | tf_op jit(solution)/shard_map/all_gather | solution.py:17
  7.9 217.1 %all-gather.6.cloned.1.call-start = ((), (), s32[]{:S(2)}) async-start(), calls=%async_computation.2 | async-start | bytes 33030144 | tf_op jit(solution)/shard_map/all_gather | solution.py:20
  8.7 272.9 %all-reduce.6.cloned.1.call-start = ((), (), s32[]{:S(2)}) async-start(), calls=%async_computation.4 | async-start | bytes 458752 | tf_op jit(solution)/shard_map/psum | solution.py:30
  9.8 236.4 %copy-start.3 = (s32[3]{0:T(128)S(1)}, s32[3]{0:T(128)}, u32[]{:S(2)}) copy-start(s32[3]{0:T(128)} %param.16) | copy-start | bytes 40
  9.8 279.1 %copy-start.2 = (s32[16]{0:T(128)S(1)}, s32[16]{0:T(128)}, u32[]{:S(2)}) copy-start(s32[16]{0:T(128)} %param.17) | copy-start | bytes 196
  285.2 28.7 %all-to-all-start = ((f32[3,8,512]{2,0,1:T(4,128)}), f32[3,8,512]{2,0,1:T(4,128)S(1)}, u32[]{:S(2)}, u32[]{:S(2)}) async-start(f32[3,8,512]{2,0,1:T(4,128)} %copy.18), calls=%async_computation | async-start | bytes 131072 | tf_op jit(solution)/shard_map/all_to_all | solution.py:51
  288.8 77.3 %all-reduce.4.cloned.1.call-start = ((), (), s32[]{:S(2)}) async-start(), calls=%async_computation.3 | async-start | bytes 524288 | tf_op jit(solution)/shard_map/psum | solution.py:44
Sparse Core Ops, SparseCore 0:
  9.6 66.1 all-gather.3
  77.6 147.3 all-gather.5
  246.3 35.2 all-reduce.5
  313.3 52.7 all-reduce.3
where the time goes:
time: 375 us
  waiting for transfers between devices  301 us (80%)
  matrix products  28.7 us (8%)
  blocking collectives  23.2 us (6%)
  between operations  14.5 us (4%)
  starting transfers between devices  3.75 us (1%)
    all_gather x1, waiting for transfers between devices, body(): lax.all_gather(down_weight, 'dp', axis=1, tiled=True)  149 us
    all_gather x1, waiting for transfers between devices, body(): full_grad = lax.all_gather(grad_out, 'tensor', axis=1, tiled=True)  66 us
    psum x1, waiting for transfers between devices, body(): query_feat, total_square = lax.psum((query_part, local_square), 'dp')  49 us
    psum x1, waiting for transfers between devices, body(): out_factor, in_factor = lax.psum((out_part, in_part), 'tensor')  35.4 us
    dot_general x1, matrix products, body(): out_part = jnp.dot(gate_grad, proj_out, preferred_element_type=jnp.float32)  20.3 us
    psum x1, blocking collectives, body(): query_feat, total_square = lax.psum((query_part, local_square), 'dp')  15 us
    all_gather x1, blocking collectives, body(): lax.all_gather(own_cols, 'dp', axis=0, tiled=True)  8.25 us
  transfers between devices with their start and end apart: 5, of which 4 were waited for; matrix products, arithmetic and copies ran while one was open for 1% of the time, Pallas kernels for 0%

commit v1 on v0

--- a/solution.py
+++ b/solution.py
@@ -14,7 +14,14 @@
     tokens_here = acts.shape[0]
     examples_here = lengths.shape[0]
     seq_len = tokens_here // examples_here
-    full_grad = lax.all_gather(grad_out, "tensor", axis=1, tiled=True)
+    ring = [grad_out]
+    for hop in range(3):
+        ring.append(lax.ppermute(ring[-1], "tensor", [(dev, (dev + 1) % 4) for dev in range(4)]))
+    full_grad = jnp.roll(
+        jnp.concatenate(ring[::-1], axis=1),
+        (lax.axis_index("tensor") + 1) * ring[0].shape[1],
+        axis=1,
+    )
     hidden_grad = lax.dot_general(
         full_grad,
         lax.all_gather(down_weight, "dp", axis=1, tiled=True),

time: 375 us -> 285 us (0.76)
  waiting for transfers between devices: 301 us -> 196 us
  local copies, waits for them, and re-layouts: 2.3 us -> 13 us
    all_gather x1, waiting for transfers between devices: 149 us -> 79.6 us  [body(): lax.all_gather(down_weight, 'dp', axis=1, tiled=True)]
    all_gather x1 -> x0, waiting for transfers between devices: 66 us -> none  [body(): full_grad = lax.all_gather(grad_out, 'tensor', axis=1, tiled=True)]
    ppermute x0 -> x3, waiting for transfers between devices: none -> 58.1 us  [body(): lax.ppermute(ring[-1], 'tensor', [(dev, (dev + 1) % 4) for dev in range(4)])]
    psum x1, waiting for transfers between devices: 49 us -> 22.3 us  [body(): query_feat, total_square = lax.psum((query_part, local_square), 'dp')]
    unnamed x12 -> x17, local copies, waits for them, and re-layouts: 0.08 us -> 9.73 us
  transfers between devices with their start and end apart: 5 -> 7, of which waited for: 4 -> 6; matrix products, arithmetic and copies ran while one was open for 1% -> 6% of each run, Pallas kernels for 0% -> 0%
where the time goes in v1:
time: 285 us; the launch traced here: 284 us
  waiting for transfers between devices  196 us (69%)
  matrix products  29.6 us (10%)
  blocking collectives  23.3 us (8%)
  between operations  14.5 us (5%)
  local copies, waits for them, and re-layouts  13 us (5%)
  starting transfers between devices  6.83 us (2%)
    all_gather x1, waiting for transfers between devices, body(): lax.all_gather(down_weight, 'dp', axis=1, tiled=True)  79.6 us
    ppermute x3, waiting for transfers between devices, body(): lax.ppermute(ring[-1], 'tensor', [(dev, (dev + 1) % 4) for dev in range(4)])  58.1 us
    psum x1, waiting for transfers between devices, body(): out_factor, in_factor = lax.psum((out_part, in_part), 'tensor')  35.3 us
    psum x1, waiting for transfers between devices, body(): query_feat, total_square = lax.psum((query_part, local_square), 'dp')  22.3 us
    dot_general x1, matrix products, body(): out_part = jnp.dot(gate_grad, proj_out, preferred_element_type=jnp.float32)  20.4 us
    psum x1, blocking collectives, body(): query_feat, total_square = lax.psum((query_part, local_square), 'dp')  15.1 us
    unnamed x17, local copies, waits for them, and re-layouts  9.73 us
    all_gather x1, blocking collectives, body(): lax.all_gather(own_cols, 'dp', axis=0, tiled=True)  8.26 us
  transfers between devices with their start and end apart: 7, of which 6 were waited for; matrix products, arithmetic and copies ran while one was open for 6% of the time, Pallas kernels for 0%

profile of v1, /device:TPU:0, one launch (start us, length us, event | category | flops | bytes accessed | tf_op | source)
XLA Modules:
  0.0 284.2 jit_solution(3515044689885996386)
XLA Ops:
  7.2 0.7 all-gather.3.cloned.1.call-update
  8.0 3.1 %collective-permute-start = (bf16[384,1024]{1,0:T(8,128)(2,1)}, bf16[384,1024]{1,0:T(8,128)(2,1)S(1)}, u32[]{:S(2)}, u32[]{:S(2)}) collective-permute-start(bf16[384,1024]{1,0:T(8,128)(2,1)} %param.10), channel_id=1, source_target_pairs={{0,1},{1,2},{2,3},{3,0},{4,5},{5,6},{6,7},{7,4},{8,9},{9,10},{10,1... | collective-permute-start | bytes 2359304 | tf_op jit(solution)/shard_map/ppermute | solution.py:19
  11.1 19.8 %collective-permute-done = bf16[384,1024]{1,0:T(8,128)(2,1)S(1)} collective-permute-done((bf16[384,1024]{1,0:T(8,128)(2,1)}, bf16[384,1024]{1,0:T(8,128)(2,1)S(1)}, u32[]{:S(2)}, u32[]{:S(2)}) %collective-permute-start) | collective-permute-done | bytes 786464 | tf_op jit(solution)/shard_map/ppermute | solution.py:19
  30.9 20.5 %collective-permute-done.1 = bf16[384,1024]{1,0:T(8,128)(2,1)S(1)} collective-permute-done((bf16[384,1024]{1,0:T(8,128)(2,1)S(1)}, bf16[384,1024]{1,0:T(8,128)(2,1)S(1)}, u32[]{:S(2)}, u32[]{:S(2)}) %collective-permute-start.1) | collective-permute-done | bytes 786464 | tf_op jit(solution)/shard_map/ppermute | solution.py:19
  51.4 1.3 convolution_bitcast_fusion
  52.6 0.6 copy.25
  53.3 17.8 %collective-permute-done.2 = bf16[384,1024]{1,0:T(8,128)(2,1)} collective-permute-done((bf16[384,1024]{1,0:T(8,128)(2,1)S(1)}, bf16[384,1024]{1,0:T(8,128)(2,1)}, u32[]{:S(2)}, u32[]{:S(2)}) %collective-permute-start.2) | collective-permute-done | bytes 786464 | tf_op jit(solution)/shard_map/ppermute | solution.py:19
  71.1 2.4 constant_dynamic-update-slice_fusion.7
  73.5 1.0 constant_dynamic-update-slice_fusion.6
  74.5 1.0 constant_dynamic-update-slice_fusion.5
  75.5 1.0 constant_dynamic-update-slice_fusion.4
  76.5 2.2 constant_dynamic-update-slice_fusion.3
  78.7 1.0 constant_dynamic-update-slice_fusion.2
  79.7 1.0 constant_dynamic-update-slice_fusion.1
  80.8 1.0 constant_dynamic-update-slice_fusion
  81.8 79.6 %all-gather.3.cloned.1.call-done = bf16[3584,4096]{1,0:T(8,128)(2,1)} async-done(((bf16[3584,512]{1,0:T(8,128)(2,1)}), bf16[3584,4096]{1,0:T(8,128)(2,1)}) %all-gather.3.cloned.1.call-update) | async-done | bytes 29360144 | tf_op jit(solution)/shard_map/all_gather | solution.py:27
  161.4 20.4 %fusion.17 = f32[384,64]{0,1:T(8,128)S(1)} fusion(bf16[3584,64]{0,1:T(8,128)(2,1)} %param.15, bf16[3584,4096]{1,0:T(8,128)(2,1)} %all-gather.3.cloned.1.call-done, bf16[384,3584]{1,0:T(8,128)(2,1)} %param.11, bf16[384,3584]{1,0:T(8,128)(2,1)} %param.12, bf16[384,8192]{1,0:T(8,128)(2,1)} %constant_dynamic-update-slice_fusion, s32[]{:T(128)S(6)} %select_n.17), kind=kOutput, calls=%fused_computation.36 | convolution fusion | flops 11466964992 | bytes 38567940 | tf_op jit(solution)/shard_map/dot_general | solution.py:35
  181.8 0.7 reshape.43
  182.6 0.1 fusion.14
  182.6 35.3 %all-reduce.6.cloned.1.call-done = (f32[3,128,64]{1,2,0:T(8,128)}, f32[3,128,64]{1,0,2:T(4,128)}) async-done(((f32[3,128,64]{1,2,0:T(8,128)}, f32[3,128,64]{1,0,2:T(4,128)}), (f32[3,128,64]{1,2,0:T(8,128)}, f32[3,128,64]{1,0,2:T(4,128)})) %all-reduce.6.cloned.1.call-update) | async-done | bytes 196624 | tf_op jit(solution)/shard_map/psum | solution.py:37
  217.9 0.9 broadcast_multiply_fusion
  218.9 1.8 multiply_reduce_fusion
  220.7 0.1 reshape.45
  220.8 0.1 all_to_all.14
  220.9 1.0 fusion.10
  221.9 0.7 copy.18
  222.6 3.6 %all-to-all-start = ((f32[3,8,512]{2,0,1:T(4,128)}), f32[3,8,512]{2,0,1:T(4,128)S(1)}, u32[]{:S(2)}, u32[]{:S(2)}) async-start(f32[3,8,512]{2,0,1:T(4,128)} %copy.18), calls=%async_computation | async-start | bytes 131072 | tf_op jit(solution)/shard_map/all_to_all | solution.py:58
  226.2 15.1 %psum.30 = f32[]{:T(128)} all-reduce(f32[]{:T(128)} %get-tuple-element.4), channel_id=1, replica_groups=mesh['dp'=8,'tensor'=4] {'dp'}, use_global_device_ids=true, to_apply=%region_3.4 | all-reduce | flops 1 | bytes 8 | tf_op jit(solution)/shard_map/psum | solution.py:51
  241.2 8.3 %all-gather = f32[8,3,1024]{2,1,0:T(4,128)S(1)} all-gather(f32[1,3,1024]{2,1,0:T(4,128)S(1)} %dynamic-slice_bitcast_fusion), channel_id=1, replica_groups=mesh['dp'=8,'tensor'=4] {'dp'}, dimensions={0}, use_global_device_ids=true | all-gather | bytes 110592 | tf_op jit(solution)/shard_map/all_gather | solution.py:61
  250.2 3.2 %multiply_divide_fusion = f32[512,1024]{1,0:T(8,128)} fusion(f32[24,512]{1,0:T(8,128)S(1)} %all_to_all.17, f32[24,1024]{1,0:T(8,128)S(1)} %reshape.47, f32[]{:T(128)S(6)} %add.50), kind=kOutput, calls=%fused_computation.11 | convolution fusion | flops 152043520 | bytes 2244612 | tf_op jit(solution)/shard_map/dot_general | solution.py:59
  253.4 22.3 %all-reduce.4.cloned.1.call-done = f32[16,4096]{1,0:T(8,128)} async-done(((f32[16,4096]{1,0:T(8,128)}), f32[16,4096]{1,0:T(8,128)}) %all-reduce.4.cloned.1.call-update) | async-done | bytes 262160 | tf_op jit(solution)/shard_map/psum | solution.py:51
  275.8 2.0 convolution_divide_fusion
  (20 shorter events, 0.3 us)
Async XLA Ops:
  7.2 44.2 %copy-start = (bf16[384,1024]{1,0:T(8,128)(2,1)S(1)}, bf16[384,1024]{1,0:T(8,128)(2,1)}, u32[]{:S(2)}) copy-start(bf16[384,1024]{1,0:T(8,128)(2,1)} %param.9) | copy-start | bytes 2359300
  7.2 68.3 %copy-start.1 = (bf16[384,1024]{1,0:T(8,128)(2,1)S(1)}, bf16[384,1024]{1,0:T(8,128)(2,1)}, u32[]{:S(2)}) copy-start(bf16[384,1024]{1,0:T(8,128)(2,1)} %param.10) | copy-start | bytes 2359300
  7.2 154.2 %all-gather.3.cloned.1.call-start = ((), (), s32[]{:S(2)}) async-start(), calls=%async_computation.1 | async-start | bytes 33030144 | tf_op jit(solution)/shard_map/all_gather | solution.py:27
  7.9 210.0 %all-reduce.6.cloned.1.call-start = ((), (), s32[]{:S(2)}) async-start(), calls=%async_computation.3 | async-start | bytes 458752 | tf_op jit(solution)/shard_map/psum | solution.py:37
  8.0 22.9 %collective-permute-start = (bf16[384,1024]{1,0:T(8,128)(2,1)}, bf16[384,1024]{1,0:T(8,128)(2,1)S(1)}, u32[]{:S(2)}, u32[]{:S(2)}) collective-permute-start(bf16[384,1024]{1,0:T(8,128)(2,1)} %param.10), channel_id=1, source_target_pairs={{0,1},{1,2},{2,3},{3,0},{4,5},{5,6},{6,7},{7,4},{8,9},{9,10},{10,1... | collective-permute-start | bytes 2359304 | tf_op jit(solution)/shard_map/ppermute | solution.py:19
  30.9 20.5 %collective-permute-start.1 = (bf16[384,1024]{1,0:T(8,128)(2,1)S(1)}, bf16[384,1024]{1,0:T(8,128)(2,1)S(1)}, u32[]{:S(2)}, u32[]{:S(2)}) collective-permute-start(bf16[384,1024]{1,0:T(8,128)(2,1)S(1)} %collective-permute-done), channel_id=1, source_target_pairs={{0,1},{1,2},{2,3},{3,0},{4,5},{5,6},{6,7},{7,4},{8,9},{9,10},{10,1... | collective-permute-start | bytes 2359304 | tf_op jit(solution)/shard_map/ppermute | solution.py:19
  51.4 19.8 %collective-permute-start.2 = (bf16[384,1024]{1,0:T(8,128)(2,1)S(1)}, bf16[384,1024]{1,0:T(8,128)(2,1)}, u32[]{:S(2)}, u32[]{:S(2)}) collective-permute-start(bf16[384,1024]{1,0:T(8,128)(2,1)S(1)} %collective-permute-done.1), channel_id=1, source_target_pairs={{0,1},{1,2},{2,3},{3,0},{4,5},{5,6},{6,7},{7,4},{8,9},{9,10},{10,1... | collective-permute-start | bytes 2359304 | tf_op jit(solution)/shard_map/ppermute | solution.py:19
  81.8 100.8 %copy-start.3 = (s32[3]{0:T(128)S(1)}, s32[3]{0:T(128)}, u32[]{:S(2)}) copy-start(s32[3]{0:T(128)} %param.16) | copy-start | bytes 40
  81.8 139.0 %copy-start.2 = (s32[16]{0:T(128)S(1)}, s32[16]{0:T(128)}, u32[]{:S(2)}) copy-start(s32[16]{0:T(128)} %param.17) | copy-start | bytes 196
  182.5 93.3 %all-reduce.4.cloned.1.call-start = ((), (), s32[]{:S(2)}) async-start(), calls=%async_computation.2 | async-start | bytes 524288 | tf_op jit(solution)/shard_map/psum | solution.py:51
  222.6 27.6 %all-to-all-start = ((f32[3,8,512]{2,0,1:T(4,128)}), f32[3,8,512]{2,0,1:T(4,128)S(1)}, u32[]{:S(2)}, u32[]{:S(2)}) async-start(f32[3,8,512]{2,0,1:T(4,128)} %copy.18), calls=%async_computation | async-start | bytes 131072 | tf_op jit(solution)/shard_map/all_to_all | solution.py:58
Sparse Core Ops, SparseCore 0:
  9.9 151.4 all-gather.2
  182.6 35.2 all-reduce.5
  222.0 53.6 all-reduce.3
